TPU v7x, 256 devices: a whole 4x4x8 slice. The times are simulated.
256 devices in a mesh: ctx: 8 (over x, y_hi), chan: 32 (over z, y_lo, core).
Axes of the slice: x: 4, y: 4 (y_hi: 2, y_lo: 2; y = y_hi * 2 + y_lo), z: 8, core: 2. Of those that a mesh axis runs over, the one named last changes fastest.
Arguments:
- inputs: bfloat16 [4096, 4096], P('ctx', 'chan'), may hold values from -6 to 6
- w_in: bfloat16 [4096, 3, 4096], P(None, None, 'chan'), may hold values from -0.09375 to 0.09375
- conv_taps: bfloat16 [3, 3, 4096], P(None, None, 'chan'), may hold values from -3.59375 to 3.59375
- skip_gain: float32 [4096], P('chan'), may hold values from 0.5 to 1.5
- filter_taps: bfloat16 [4096, 4096], P('ctx', 'chan'), may hold values from -0.09375 to 0.09375
- w_out: bfloat16 [4096, 4096], P('chan'), may hold values from -0.1875 to 0.1875
Outputs:
- result: bfloat16 [4096, 4096], P('ctx', 'chan')
All inputs are finite; a program needn't handle non-finite values.
Results may differ from a plain program's by a relative error of at most 0.024.
Values may be sent and summed in bfloat16 or wider, within the bound.
A program may use at most 64 MiB of HBM per device.

v0:
```python
import math
import jax
import jax.numpy as jnp
from jax import lax
from jax.sharding import PartitionSpec as P

KERNEL = 3


def from_behind(block, axis, distance):
    devices = range(lax.axis_size(axis))
    route = [(i - distance, i) for i in devices if i - distance in devices]
    return lax.ppermute(block, axis, route)


def angles(row_count, col_count, double_len):
    row_ids = jnp.arange(row_count, dtype=jnp.int32)[:, None]
    col_ids = jnp.arange(col_count, dtype=jnp.int32)[None, :]
    return 2.0 * math.pi / double_len * (row_ids * col_ids % double_len).astype(jnp.float32)


def tables(span_len):
    double_len = 2 * span_len
    first = angles(double_len, span_len, double_len)
    forward_in = jnp.concatenate([jnp.cos(first), -jnp.sin(first)], 0).astype(jnp.bfloat16)
    second = angles(double_len, double_len, double_len)
    forward_taps = jnp.concatenate([jnp.cos(second), -jnp.sin(second)], 0).astype(jnp.bfloat16)
    third = angles(span_len, double_len, double_len)
    inverse = (jnp.concatenate([jnp.cos(third), -jnp.sin(third)], 1) / double_len).astype(
        jnp.bfloat16
    )
    return (forward_in, forward_taps, inverse)


def body(inputs, w_in, conv_taps, skip_gain, filter_taps, w_out):
    span_len, width_dev = inputs.shape
    double_len = 2 * span_len
    groups = lax.axis_size("ctx")
    position = lax.axis_index("ctx")
    w_flat = w_in.reshape(w_in.shape[0], 3 * width_dev)
    projected = jnp.dot(
        lax.all_gather(inputs, "chan", axis=1, tiled=True),
        w_flat,
        preferred_element_type=jnp.float32,
    )
    by_stream = projected.astype(jnp.bfloat16).reshape(span_len, 3, width_dev)
    rim_rows = from_behind(by_stream[span_len - (KERNEL - 1) :], "ctx", 1)
    padded = jnp.concatenate([rim_rows, by_stream], 0)
    filtered = jnp.zeros((span_len, 3, width_dev), jnp.float32)
    for lag in range(KERNEL):
        start_row = KERNEL - 1 - lag
        filtered = filtered + conv_taps[lag].astype(jnp.float32) * padded[
            start_row : start_row + span_len
        ].astype(jnp.float32)
    streams = filtered.astype(jnp.bfloat16)
    gate_out = streams[:, 0]
    gated_in = (streams[:, 1].astype(jnp.float32) * streams[:, 2].astype(jnp.float32)).astype(
        jnp.bfloat16
    )
    forward_in, forward_taps, inverse = tables(span_len)
    all_taps = lax.all_gather(filter_taps[None], "ctx", axis=0, tiled=True)
    previous = jnp.concatenate(
        [jnp.zeros((1, span_len, width_dev), jnp.bfloat16), all_taps[:-1]], 0
    )
    padded_taps = jnp.concatenate(
        [all_taps, jnp.zeros((groups, 1, width_dev), jnp.bfloat16), previous[:, 1:]], 1
    )
    spectra_taps = jnp.einsum(
        "fm,kmd->kfd", forward_taps, padded_taps, preferred_element_type=jnp.float32
    ).astype(jnp.bfloat16)

    def accumulate(spectra):
        pieces = spectra.shape[0]
        lag_index = position - jnp.arange(pieces, dtype=jnp.int32)
        causal = lag_index >= 0
        chosen = jnp.take(spectra_taps, jnp.clip(lag_index, 0, groups - 1), axis=0)
        real_g = chosen[:, :double_len].astype(jnp.float32)
        imag_g = chosen[:, double_len:].astype(jnp.float32)
        real_u = spectra[:, :double_len].astype(jnp.float32)
        imag_u = spectra[:, double_len:].astype(jnp.float32)
        product = jnp.concatenate(
            [real_g * real_u - imag_g * imag_u, real_g * imag_u + imag_g * real_u], 1
        )
        product = jnp.where(causal[:, None, None], product, 0.0)
        return jnp.sum(product, axis=0)

    empty = jnp.zeros((2 * double_len, width_dev), jnp.float32)
    incoming = lax.all_gather(gated_in[None], "ctx", axis=0, tiled=True)

    def transform(current):
        spectra = jnp.einsum(
            "fb,mbc->mfc", forward_in, incoming, preferred_element_type=jnp.float32
        ).astype(jnp.bfloat16)
        return accumulate(spectra)

    def unchanged(current):
        return current

    mixture = lax.cond(jnp.int32(0) <= position, transform, unchanged, empty)
    long_out = jnp.dot(inverse, mixture.astype(jnp.bfloat16), preferred_element_type=jnp.float32)
    long_out = long_out + skip_gain * gated_in.astype(jnp.float32)
    gated_out = (gate_out.astype(jnp.float32) * long_out).astype(jnp.bfloat16)
    shares = lax.psum_scatter(
        lax.dot_general(
            w_out, gated_out, (((0,), (1,)), ((), ())), preferred_element_type=jnp.float32
        ).astype(jnp.bfloat16),
        "chan",
        scatter_dimension=0,
        tiled=True,
    ).astype(jnp.float32)
    result = shares.T.astype(jnp.bfloat16)
    return result


def solution(mesh):
    return jax.shard_map(
        body,
        mesh=mesh,
        in_specs=(
            P("ctx", "chan"),
            P(None, None, "chan"),
            P(None, None, "chan"),
            P("chan"),
            P("ctx", "chan"),
            P("chan", None),
        ),
        out_specs=P("ctx", "chan"),
        check_vma=False,
    )
```

profile of v0, /device:TPU:2, one launch (start us, length us, event | category | flops | bytes accessed | tf_op | source)
XLA Modules:
  0.0 362.8 jit_solution(12032733363743126009)
XLA Ops:
  6.5 0.0 copy-start
  6.5 0.0 all-gather.6.cloned.1.call-start
  6.5 0.7 all-gather.6.cloned.1.call-update
  7.3 0.0 all-gather.8.cloned.1.call-start
  7.3 0.7 all-gather.8.cloned.1.call-update
  8.0 0.0 all-gather.10.cloned.1.call-start
  8.1 4.8 %copy.23 = bf16[4096,3,128]{0,2,1:T(8,128)(2,1)} copy(bf16[4096,3,128]{2,0,1:T(8,128)(2,1)} %param.9) | data formatting | bytes 6291456 | tf_op args[1]
  12.8 9.3 %negate_convert_fusion.1 = (bf16[1024,512]{1,0:T(8,128)(2,1)}, bf16[1024,512]{1,0:T(8,128)(2,1)}) fusion(), kind=kLoop, calls=%fused_computation.56 | loop fusion | flops 8912896 | bytes 2097152 | tf_op jit(solution)/shard_map/convert.8
  22.1 62.3 %all-gather.6.cloned.1.call-done = bf16[512,4096]{1,0:T(8,128)(2,1)} async-done(((bf16[512,128]{1,0:T(8,128)(2,1)}), bf16[512,4096]{1,0:T(8,128)(2,1)}) %all-gather.6.cloned.1.call-update) | async-done | bytes 4194320 | tf_op jit(solution)/shard_map/all_gather | solution.py:42
  84.4 0.0 copy-start.2
  84.4 5.5 %convolution_convert_fusion.1 = bf16[512,384]{1,0:T(8,128)(2,1)S(1)} fusion(bf16[512,4096]{1,0:T(8,128)(2,1)} %all-gather.6.cloned.1.call-done, bf16[4096,384]{0,1:T(8,128)(2,1)} %bitcast.54), kind=kOutput, calls=%fused_computation.66 | convolution fusion | flops 1610809344 | bytes 7733248 | tf_op jit(solution)/shard_map/dot_general | solution.py:41
  89.9 4.9 %collective-permute-start = (bf16[2,3,128]{2,0,1:T(2,128)(2,1)S(1)}, bf16[2,3,128]{2,0,1:T(2,128)(2,1)S(1)}, u32[]{:S(2)}, u32[]{:S(2)}) collective-permute-start(bf16[2,3,128]{2,0,1:T(2,128)(2,1)S(1)} %slice_bitcast_fusion.2), channel_id=1, source_target_pairs={{0,32},{32,64},{64,96},{96,128},{128,160},{160,192},{192,224},{1,3... | collective-permute-start | bytes 4616 | tf_op jit(solution)/shard_map/ppermute | solution.py:13
  94.9 0.0 copy-done.2
  94.9 0.2 copy.24
  95.1 0.2 copy.25
  95.3 2.5 collective-permute-done
  97.8 0.3 add_convert_fusion
  98.1 0.7 multiply_convert_fusion
  98.8 0.0 all-gather.10.cloned.1.call-update
  98.8 0.2 reduce-scatter.4.cloned.1.call-start
  99.0 9.1 %sine_negate_fusion = (f32[512,1024]{1,0:T(8,128)S(1)}, f32[512,1024]{1,0:T(8,128)}) fusion(), kind=kLoop, calls=%fused_computation.60 | loop fusion | flops 7864320 | bytes 4194304 | tf_op jit(solution)/shard_map/neg | solution.py:29
  108.2 3.0 pad_maximum_fusion
  111.1 17.8 %negate_convert_fusion = (bf16[1024,1024]{1,0:T(8,128)(2,1)}, bf16[1024,1024]{1,0:T(8,128)(2,1)}) fusion(), kind=kLoop, calls=%fused_computation.34 | loop fusion | flops 17825792 | bytes 4194304 | tf_op jit(solution)/shard_map/convert.6
  129.0 8.9 %all-gather.8.cloned.1.call-done = bf16[4096,128]{1,0:T(8,128)(2,1)} async-done(((bf16[512,128]{1,0:T(8,128)(2,1)}), bf16[4096,128]{1,0:T(8,128)(2,1)}) %all-gather.8.cloned.1.call-update) | async-done | bytes 1048592 | tf_op jit(solution)/shard_map/all_gather | solution.py:61
  137.9 2.2 slice.71
  140.0 2.3 copy.28
  142.3 2.3 copy.29
  144.6 1.6 pad_slice_fusion
  146.2 9.1 %convert_bitcast_fusion.1 = bf16[8,2048,128]{1,2,0:T(8,128)(2,1)} fusion(bf16[1024,1024]{1,0:T(8,128)(2,1)} %get-tuple-element.40, bf16[1024,1024]{1,0:T(8,128)(2,1)} %get-tuple-element.41, bf16[8,511,128]{1,2,0:T(8,128)(2,1)S(1)} %pad_slice_fusion, bf16[8,512,128]{1,2,0:T(8,128)(2,1)} %copy.29, bf16[1024]{0:T(1024)(128)(2,1)S(1)} %pad.8.clone), kind=kOutput, calls=%fused_computation.33 | convolution fusion | flops 4311744512 | bytes 10485760 | tf_op jit(solution)/shard_map/fm,kmd->kfd/dot_general | solution.py:68
  155.2 36.6 %all-gather.10.cloned.1.call-done = bf16[4096,1,128]{2,0,1:T(8,128)(2,1)} async-done(((bf16[512,1,128]{2,0,1:T(8,128)(2,1)}), bf16[4096,1,128]{2,0,1:T(8,128)(2,1)}) %all-gather.10.cloned.1.call-update) | async-done | bytes 1048592 | tf_op jit(solution)/shard_map/all_gather | solution.py:88
  191.8 0.0 copy-start.3
  191.8 28.0 %conditional.1 = (bf16[2048,128]{0,1:T(8,128)(2,1)}) conditional(s32[]{:T(128)} %convert_element_type.147, () %tuple.13, (s32[]{:T(128)}, bf16[8,2048,128]{1,2,0:T(8,128)(2,1)}, bf16[8,512,128]{2,1,0:T(8,128)(2,1)}, bf16[2048,512]{1,0:T(8,128)(2,1)}) %tuple.35), branch_computations={%region_0.1_spmd, %region_1.3_spmd} | conditional | flops 2168194048 | bytes 79171784 | solution.py:99
  191.9 6.5 %copy.30 = bf16[8,2048,128]{2,1,0:T(8,128)(2,1)} copy(bf16[8,2048,128]{1,2,0:T(8,128)(2,1)} %get-tuple-element.30) | data formatting | bytes 8388608 | tf_op jit(solution)/shard_map
  198.3 5.2 %gather_fusion = bf16[8,2048,128]{2,1,0:T(8,128)(2,1)} fusion(bf16[8,2048,128]{2,1,0:T(8,128)(2,1)} %copy.30, s32[1024]{0:T(1024)S(1)} %pad_clamp_fusion), kind=kCustom, calls=%fused_computation | custom fusion | bytes 8388640 | tf_op jit(solution)/shard_map/cond/branch_1_fun/jit(_take)/gather | solution.py:76
  203.6 6.5 %copy.22 = bf16[8,2048,128]{1,2,0:T(8,128)(2,1)} copy(bf16[8,2048,128]{2,1,0:T(8,128)(2,1)} %gather_fusion) | data formatting | bytes 8388608 | tf_op jit(solution)/shard_map/cond/branch_1_fun/jit(_take)/gather | solution.py:76
  210.1 2.8 broadcast_select_fusion
  212.9 0.0 copy-done.1
  213.0 0.3 copy-done.4
  213.2 2.4 convert_bitcast_fusion
  215.6 2.1 fusion.1
  217.8 2.1 fusion
  219.8 0.0 copy-done
  219.8 0.0 copy-done.3
  219.8 5.5 %fusion.6 = bf16[4096,512]{0,1:T(8,128)(2,1)} fusion(bf16[128,4096]{1,0:T(8,128)(2,1)S(1)} %copy-done, bf16[2048,128]{0,1:T(8,128)(2,1)} %get-tuple-element.46, f32[512,1024]{1,0:T(8,128)S(1)} %get-tuple-element.44, f32[512,1024]{1,0:T(8,128)} %get-tuple-element.45, bf16[512,3,128]{2,0,1:T(8,128)(2,1)S(1)} %add_convert_fusion, ...), kind=kOutput, calls=%fused_computation.23 | convolution fusion | flops 810942464 | bytes 10224128 | tf_op jit(solution)/shard_map/dot_general | solution.py:104
  225.4 6.5 %copy.33 = bf16[4096,512]{1,0:T(8,128)(2,1)} copy(bf16[4096,512]{0,1:T(8,128)(2,1)} %fusion.6) | data formatting | bytes 8388608
  231.9 0.0 reduce-scatter.4.cloned.1.call-update
  231.9 122.7 %reduce-scatter.4.cloned.1.call-done = bf16[128,512]{1,0:T(8,128)(2,1)} async-done(((bf16[4096,512]{1,0:T(8,128)(2,1)}), bf16[128,512]{1,0:T(8,128)(2,1)}) %reduce-scatter.4.cloned.1.call-update) | async-done | bytes 131088
  354.6 1.7 copy.34
  (8 shorter events, 0.0 us)
Async XLA Ops:
  6.5 213.3 %copy-start = (bf16[128,4096]{1,0:T(8,128)(2,1)S(1)}, bf16[128,4096]{1,0:T(8,128)(2,1)}, u32[]{:S(2)}) copy-start(bf16[128,4096]{1,0:T(8,128)(2,1)} %param.13) | copy-start | bytes 3145732
  6.5 77.8 %all-gather.6.cloned.1.call-start = ((), (), s32[]{:S(2)}) async-start(), calls=%async_computation.1 | async-start | bytes 4325376 | tf_op jit(solution)/shard_map/all_gather | solution.py:42
  7.3 130.6 %all-gather.8.cloned.1.call-start = ((), (), s32[]{:S(2)}) async-start(), calls=%async_computation.2 | async-start | bytes 1179648 | tf_op jit(solution)/shard_map/all_gather | solution.py:61
  8.0 183.8 %all-gather.10.cloned.1.call-start = ((), (), s32[]{:S(2)}) async-start(), calls=%async_computation.3 | async-start | bytes 1179648 | tf_op jit(solution)/shard_map/all_gather | solution.py:88
  84.4 10.5 %copy-start.2 = (bf16[3,3,128]{2,1,0:T(4,128)(2,1)S(1)}, bf16[3,3,128]{2,1,0:T(4,128)(2,1)}, u32[]{:S(2)}) copy-start(bf16[3,3,128]{2,1,0:T(4,128)(2,1)} %param.10) | copy-start | bytes 6916
  89.9 7.9 %collective-permute-start = (bf16[2,3,128]{2,0,1:T(2,128)(2,1)S(1)}, bf16[2,3,128]{2,0,1:T(2,128)(2,1)S(1)}, u32[]{:S(2)}, u32[]{:S(2)}) collective-permute-start(bf16[2,3,128]{2,0,1:T(2,128)(2,1)S(1)} %slice_bitcast_fusion.2), channel_id=1, source_target_pairs={{0,32},{32,64},{64,96},{96,128},{128,160},{160,192},{192,224},{1,3... | collective-permute-start | bytes 4616 | tf_op jit(solution)/shard_map/ppermute | solution.py:13
  98.8 255.8 %reduce-scatter.4.cloned.1.call-start = ((), (), s32[]{:S(2)}) async-start(), calls=%async_computation.4 | async-start | bytes 4325376
  191.8 28.0 %copy-start.3 = (f32[128]{0:T(128)S(1)}, f32[128]{0:T(128)}, u32[]{:S(2)}) copy-start(f32[128]{0:T(128)} %param.11) | copy-start | bytes 1540
  210.1 2.9 copy-start.1
  210.1 3.1 copy-start.4
Sparse Core Ops, SparseCore 0:
  9.1 75.2 all-gather.5
  87.0 50.7 all-gather.7
  140.5 51.2 all-gather.9
  232.0 122.5 reduce-scatter.3
where the time goes:
time: 364 us; the launch traced here: 363 us
  waiting for transfers between devices  234 us (64%)
  other arithmetic  47.2 us (13%)
  local copies, waits for them, and re-layouts  40.2 us (11%)
  matrix products  22.5 us (6%)
  between operations  13.2 us (4%)
  starting transfers between devices  5.22 us (1%)
    unnamed x5, waiting for transfers between devices  124 us
    all_gather x1, waiting for transfers between devices, body(): lax.all_gather(inputs, 'chan', axis=1, tiled=True)  62.3 us
    all_gather x1, waiting for transfers between devices, body(): incoming = lax.all_gather(gated_in[None], 'ctx', axis=0, tiled=True)  36.6 us
    another operation x2, other arithmetic  27.1 us
    unnamed x9, local copies, waits for them, and re-layouts  13 us
    gather x2, local copies, waits for them, and re-layouts, accumulate(): chosen = jnp.take(spectra_taps, jnp.clip(lag_index, 0, groups - 1), axis=0)  11.8 us
    neg x1, other arithmetic, tables(): -jnp.sin(third)  9.1 us
    dot_general x1, matrix products, body(): jnp.einsum('fm,kmd->kfd', forward_taps, padded_taps, preferred_element_ty...  9.05 us
  transfers between devices with their start and end apart: 5, of which 5 were waited for; matrix products, arithmetic and copies ran while one was open for 19% of the time, Pallas kernels for 0%

commit v1 on v0

--- a/solution.py
+++ b/solution.py
@@ -5,6 +5,13 @@
 from jax.sharding import PartitionSpec as P
 
 KERNEL = 3
+
+
+def gather_over(shard, name, d):
+    count = lax.axis_size(name)
+    blocks = jnp.stack([shard for _ in range(count)])
+    blocks = lax.all_to_all(blocks, name, split_axis=0, concat_axis=0)
+    return jnp.concatenate(blocks, axis=d)
 
 
 def from_behind(block, axis, distance):
@@ -38,11 +45,7 @@
     groups = lax.axis_size("ctx")
     position = lax.axis_index("ctx")
     w_flat = w_in.reshape(w_in.shape[0], 3 * width_dev)
-    projected = jnp.dot(
-        lax.all_gather(inputs, "chan", axis=1, tiled=True),
-        w_flat,
-        preferred_element_type=jnp.float32,
-    )
+    projected = jnp.dot(gather_over(inputs, "chan", 1), w_flat, preferred_element_type=jnp.float32)
     by_stream = projected.astype(jnp.bfloat16).reshape(span_len, 3, width_dev)
     rim_rows = from_behind(by_stream[span_len - (KERNEL - 1) :], "ctx", 1)
     padded = jnp.concatenate([rim_rows, by_stream], 0)

time: 364 us -> 351 us (0.964)
  waiting for transfers between devices: 234 us -> 207 us
  starting transfers between devices: 5.22 us -> 15.1 us
  local copies, waits for them, and re-layouts: 40.2 us -> 43.9 us
    all_to_all x0 -> x1, waiting for transfers between devices: none -> 81.9 us  [gather_over(): blocks = lax.all_to_all(blocks, name, split_axis=0, concat_axis=0)]
    all_gather x1 -> x0, waiting for transfers between devices: 62.3 us -> none  [body(): lax.all_gather(inputs, 'chan', axis=1, tiled=True)]
    all_gather x1, waiting for transfers between devices: 36.6 us -> 0.01 us  [body(): incoming = lax.all_gather(gated_in[None], 'ctx', axis=0, tiled=True)]
    all_to_all x0 -> x1, starting transfers between devices: none -> 10 us  [gather_over(): blocks = lax.all_to_all(blocks, name, split_axis=0, concat_axis=0)]
    all_gather x1, waiting for transfers between devices: 8.9 us -> 0.01 us  [body(): all_taps = lax.all_gather(filter_taps[None], 'ctx', axis=0, tiled=True)]
    another operation x1 -> x2, local copies, waits for them, and re-layouts: 6.46 us -> 8.9 us
    unnamed x5 -> x4, waiting for transfers between devices: 124 us -> 123 us
    unnamed x9 -> x10, local copies, waits for them, and re-layouts: 13 us -> 14.1 us
  transfers between devices with their start and end apart: 5 -> 5, of which waited for: 5 -> 3; matrix products, arithmetic and copies ran while one was open for 19% -> 20% of each run, Pallas kernels for 0% -> 0%
where the time goes in v1:
time: 351 us; the launch traced here: 350 us
  waiting for transfers between devices  207 us (59%)
  other arithmetic  47.2 us (13%)
  local copies, waits for them, and re-layouts  43.9 us (13%)
  matrix products  22.7 us (6%)
  starting transfers between devices  15.1 us (4%)
  between operations  13.2 us (4%)
    unnamed x4, waiting for transfers between devices  123 us
    all_to_all x1, waiting for transfers between devices, gather_over(): blocks = lax.all_to_all(blocks, name, split_axis=0, concat_axis=0)  81.9 us
    another operation x2, other arithmetic  27.1 us
    unnamed x10, local copies, waits for them, and re-layouts  14.1 us
    gather x2, local copies, waits for them, and re-layouts, accumulate(): chosen = jnp.take(spectra_taps, jnp.clip(lag_index, 0, groups - 1), axis=0)  11.8 us
    all_to_all x1, starting transfers between devices, gather_over(): blocks = lax.all_to_all(blocks, name, split_axis=0, concat_axis=0)  10 us
    dot_general x1, matrix products, body(): jnp.einsum('fm,kmd->kfd', forward_taps, padded_taps, preferred_element_ty...  9.15 us
    neg x1, other arithmetic, tables(): -jnp.sin(third)  9.09 us
  transfers between devices with their start and end apart: 5, of which 3 were waited for; matrix products, arithmetic and copies ran while one was open for 20% of the time, Pallas kernels for 0%

profile of v1, /device:TPU:2, one launch (start us, length us, event | category | flops | bytes accessed | tf_op | source)
XLA Modules:
  0.0 349.6 jit_solution(4743522002742137915)
XLA Ops:
  6.5 0.0 copy-start
  6.5 1.1 copy.25
  7.6 2.4 stack.2
  10.1 10.0 %all-to-all-start = ((bf16[32,512,128]{1,2,0:T(8,128)(2,1)}), bf16[32,512,128]{1,2,0:T(8,128)(2,1)}, u32[]{:S(2)}, u32[]{:S(2)}) async-start(bf16[32,512,128]{1,2,0:T(8,128)(2,1)} %stack.2), calls=%async_computation | async-start | bytes 8388608 | tf_op jit(solution)/shard_map/all_to_all | solution.py:13
  20.1 0.0 all-gather.5.cloned.1.call-start
  20.1 0.7 all-gather.5.cloned.1.call-update
  20.8 0.0 all-gather.7.cloned.1.call-start
  20.9 4.7 %copy.26 = bf16[4096,3,128]{0,2,1:T(8,128)(2,1)} copy(bf16[4096,3,128]{2,0,1:T(8,128)(2,1)} %param.9) | data formatting | bytes 6291456 | tf_op args[1]
  25.6 9.3 %negate_convert_fusion.1 = (bf16[1024,512]{1,0:T(8,128)(2,1)}, bf16[1024,512]{1,0:T(8,128)(2,1)}) fusion(), kind=kLoop, calls=%fused_computation.56 | loop fusion | flops 8912896 | bytes 2097152 | tf_op jit(solution)/shard_map/convert.8
  34.9 81.9 %all-to-all-done = bf16[32,512,128]{1,2,0:T(8,128)(2,1)} async-done(((bf16[32,512,128]{1,2,0:T(8,128)(2,1)}), bf16[32,512,128]{1,2,0:T(8,128)(2,1)}, u32[]{:S(2)}, u32[]{:S(2)}) %all-to-all-start) | async-done | bytes 4194336 | tf_op jit(solution)/shard_map/all_to_all | solution.py:13
  116.8 0.0 copy-start.2
  116.8 5.5 %convolution_convert_fusion.1 = bf16[512,384]{1,0:T(8,128)(2,1)S(1)} fusion(bf16[512,4096]{0,1:T(8,128)(2,1)} %bitcast.5, bf16[4096,384]{0,1:T(8,128)(2,1)} %bitcast.57), kind=kOutput, calls=%fused_computation.66 | convolution fusion | flops 1610809344 | bytes 7733248 | tf_op jit(solution)/shard_map/dot_general | solution.py:48
  122.3 4.8 %collective-permute-start = (bf16[2,3,128]{2,0,1:T(2,128)(2,1)S(1)}, bf16[2,3,128]{2,0,1:T(2,128)(2,1)S(1)}, u32[]{:S(2)}, u32[]{:S(2)}) collective-permute-start(bf16[2,3,128]{2,0,1:T(2,128)(2,1)S(1)} %slice_bitcast_fusion.2), channel_id=1, source_target_pairs={{0,32},{32,64},{64,96},{96,128},{128,160},{160,192},{192,224},{1,3... | collective-permute-start | bytes 4616 | tf_op jit(solution)/shard_map/ppermute | solution.py:20
  127.2 0.0 copy-done.2
  127.2 0.2 copy.27
  127.4 0.2 copy.28
  127.6 2.6 collective-permute-done
  130.2 0.3 add_convert_fusion
  130.5 0.7 multiply_convert_fusion
  131.2 0.0 all-gather.7.cloned.1.call-update
  131.2 0.2 reduce-scatter.4.cloned.1.call-start
  131.5 9.1 %sine_negate_fusion = (f32[512,1024]{1,0:T(8,128)S(1)}, f32[512,1024]{1,0:T(8,128)}) fusion(), kind=kLoop, calls=%fused_computation.60 | loop fusion | flops 7864320 | bytes 4194304 | tf_op jit(solution)/shard_map/neg | solution.py:36
  140.6 3.0 pad_maximum_fusion
  143.6 17.8 %negate_convert_fusion = (bf16[1024,1024]{1,0:T(8,128)(2,1)}, bf16[1024,1024]{1,0:T(8,128)(2,1)}) fusion(), kind=kLoop, calls=%fused_computation.34 | loop fusion | flops 17825792 | bytes 4194304 | tf_op jit(solution)/shard_map/convert.6
  161.4 0.0 all-gather.5.cloned.1.call-done
  161.4 2.3 slice.71
  163.7 2.3 copy.31
  166.0 2.3 copy.32
  168.3 1.6 pad_slice_fusion
  169.8 9.1 %convert_bitcast_fusion.1 = bf16[8,2048,128]{1,2,0:T(8,128)(2,1)} fusion(bf16[1024,1024]{1,0:T(8,128)(2,1)} %get-tuple-element.40, bf16[1024,1024]{1,0:T(8,128)(2,1)} %get-tuple-element.41, bf16[8,511,128]{1,2,0:T(8,128)(2,1)S(1)} %pad_slice_fusion, bf16[8,512,128]{1,2,0:T(8,128)(2,1)} %copy.32, bf16[1024]{0:T(1024)(128)(2,1)S(1)} %pad.8.clone), kind=kOutput, calls=%fused_computation.33 | convolution fusion | flops 4311744512 | bytes 10485760 | tf_op jit(solution)/shard_map/fm,kmd->kfd/dot_general | solution.py:71
  179.0 0.0 all-gather.7.cloned.1.call-done
  179.0 28.1 %conditional.1 = (bf16[2048,128]{0,1:T(8,128)(2,1)}) conditional(s32[]{:T(128)} %convert_element_type.147, () %tuple.13, (s32[]{:T(128)}, bf16[8,2048,128]{1,2,0:T(8,128)(2,1)}, bf16[8,512,128]{2,1,0:T(8,128)(2,1)}, bf16[2048,512]{1,0:T(8,128)(2,1)}) %tuple.33), branch_computations={%region_0.1_spmd, %region_1.3_spmd} | conditional | flops 2168194048 | bytes 79171784 | solution.py:102
  179.0 6.5 %copy.33 = bf16[8,2048,128]{2,1,0:T(8,128)(2,1)} copy(bf16[8,2048,128]{1,2,0:T(8,128)(2,1)} %get-tuple-element.30) | data formatting | bytes 8388608 | tf_op jit(solution)/shard_map
  185.5 5.4 %gather_fusion = bf16[8,2048,128]{2,1,0:T(8,128)(2,1)} fusion(bf16[8,2048,128]{2,1,0:T(8,128)(2,1)} %copy.33, s32[1024]{0:T(1024)S(1)} %pad_clamp_fusion), kind=kCustom, calls=%fused_computation | custom fusion | bytes 8388640 | tf_op jit(solution)/shard_map/cond/branch_1_fun/jit(_take)/gather | solution.py:79
  190.9 6.5 %copy.24 = bf16[8,2048,128]{1,2,0:T(8,128)(2,1)} copy(bf16[8,2048,128]{2,1,0:T(8,128)(2,1)} %gather_fusion) | data formatting | bytes 8388608 | tf_op jit(solution)/shard_map/cond/branch_1_fun/jit(_take)/gather | solution.py:79
  197.3 2.8 broadcast_select_fusion
  200.1 0.0 copy-done.1
  200.2 0.3 copy-done.4
  200.5 2.4 convert_bitcast_fusion
  202.8 2.1 fusion.1
  205.0 2.1 fusion
  207.1 0.0 copy-done
  207.1 0.0 copy-done.3
  207.1 5.6 %fusion.6 = bf16[4096,512]{0,1:T(8,128)(2,1)} fusion(bf16[128,4096]{1,0:T(8,128)(2,1)S(1)} %copy-done, bf16[2048,128]{0,1:T(8,128)(2,1)} %get-tuple-element.46, f32[512,1024]{1,0:T(8,128)S(1)} %get-tuple-element.44, f32[512,1024]{1,0:T(8,128)} %get-tuple-element.45, bf16[512,3,128]{2,0,1:T(8,128)(2,1)S(1)} %add_convert_fusion, ...), kind=kOutput, calls=%fused_computation.23 | convolution fusion | flops 810942464 | bytes 10224128 | tf_op jit(solution)/shard_map/dot_general | solution.py:107
  212.7 6.6 %copy.36 = bf16[4096,512]{1,0:T(8,128)(2,1)} copy(bf16[4096,512]{0,1:T(8,128)(2,1)} %fusion.6) | data formatting | bytes 8388608
  219.3 0.0 reduce-scatter.4.cloned.1.call-update
  219.3 122.1 %reduce-scatter.4.cloned.1.call-done = bf16[128,512]{1,0:T(8,128)(2,1)} async-done(((bf16[4096,512]{1,0:T(8,128)(2,1)}), bf16[128,512]{1,0:T(8,128)(2,1)}) %reduce-scatter.4.cloned.1.call-update) | async-done | bytes 131088
  341.4 1.7 copy.37
  (9 shorter events, 0.1 us)
Async XLA Ops:
  6.5 200.5 %copy-start = (bf16[128,4096]{1,0:T(8,128)(2,1)S(1)}, bf16[128,4096]{1,0:T(8,128)(2,1)}, u32[]{:S(2)}) copy-start(bf16[128,4096]{1,0:T(8,128)(2,1)} %param.13) | copy-start | bytes 3145732
  10.1 106.7 %all-to-all-start = ((bf16[32,512,128]{1,2,0:T(8,128)(2,1)}), bf16[32,512,128]{1,2,0:T(8,128)(2,1)}, u32[]{:S(2)}, u32[]{:S(2)}) async-start(bf16[32,512,128]{1,2,0:T(8,128)(2,1)} %stack.2), calls=%async_computation | async-start | bytes 8388608 | tf_op jit(solution)/shard_map/all_to_all | solution.py:13
  20.1 141.3 %all-gather.5.cloned.1.call-start = ((), (), s32[]{:S(2)}) async-start(), calls=%async_computation.2 | async-start | bytes 1179648 | tf_op jit(solution)/shard_map/all_gather | solution.py:64
  20.8 158.2 %all-gather.7.cloned.1.call-start = ((), (), s32[]{:S(2)}) async-start(), calls=%async_computation.3 | async-start | bytes 1179648 | tf_op jit(solution)/shard_map/all_gather | solution.py:91
  116.8 10.4 %copy-start.2 = (bf16[3,3,128]{2,1,0:T(4,128)(2,1)S(1)}, bf16[3,3,128]{2,1,0:T(4,128)(2,1)}, u32[]{:S(2)}) copy-start(bf16[3,3,128]{2,1,0:T(4,128)(2,1)} %param.10) | copy-start | bytes 6916
  122.3 7.9 %collective-permute-start = (bf16[2,3,128]{2,0,1:T(2,128)(2,1)S(1)}, bf16[2,3,128]{2,0,1:T(2,128)(2,1)S(1)}, u32[]{:S(2)}, u32[]{:S(2)}) collective-permute-start(bf16[2,3,128]{2,0,1:T(2,128)(2,1)S(1)} %slice_bitcast_fusion.2), channel_id=1, source_target_pairs={{0,32},{32,64},{64,96},{96,128},{128,160},{160,192},{192,224},{1,3... | collective-permute-start | bytes 4616 | tf_op jit(solution)/shard_map/ppermute | solution.py:20
  131.2 210.1 %reduce-scatter.4.cloned.1.call-start = ((), (), s32[]{:S(2)}) async-start(), calls=%async_computation.4 | async-start | bytes 4325376
  179.0 28.1 %copy-start.3 = (f32[128]{0:T(128)S(1)}, f32[128]{0:T(128)}, u32[]{:S(2)}) copy-start(f32[128]{0:T(128)} %param.11) | copy-start | bytes 1540
  197.3 2.9 copy-start.1
  197.3 3.1 copy-start.4
Sparse Core Ops, SparseCore 0:
  23.6 56.7 all-gather.4
  131.3 47.5 all-gather.6
  219.4 121.9 reduce-scatter.3
